TPU v7x, 32 devices: a whole 2x2x4 slice. The times are simulated.
32 devices in a mesh: grp: 2 (over y), orient: 4 (over z), rows: 4 (over x, core).
Axes of the slice: x: 2, y: 2, z: 4, core: 2. Of those that a mesh axis runs over, the one named last changes fastest.
Arguments:
- micrograph: bfloat16 [1024, 512], P(('grp', 'rows')), parts along dimension 0, may hold values from -6 to 6
- bank: bfloat16 [20, 512, 512], P(None, 'rows'), may hold values from -0.01171875 to 0.01171875
- orient_index: int32 [16], P('orient'), may hold values from 0 to 19
- noise_power: float32 [1024, 512], P('grp'), parts along dimension 0, may hold values from 0.25 to 4
- defocus: float32 [2], P('grp'), parts along dimension 0, may hold values from 150 to 300
Outputs:
- peak: float32 [1024, 512], P(('grp', 'rows'), 'orient'), parts along dimension 0
- total: float32 [1024, 512], P(('grp', 'rows'), 'orient'), parts along dimension 0
- squares: float32 [1024, 512], P(('grp', 'rows'), 'orient'), parts along dimension 0
There are 2 independent parts, one for each index of `grp`. A program takes and returns all parts, laid end to end along the dimension named above; an argument that names none is the same for every part. Nothing has to cross between parts.
All inputs are finite; a program needn't handle non-finite values.
Results may differ from a plain program's by a relative error of at most 0.0077.
Values may be sent and summed in bfloat16 or wider, within the bound.
A program may use at most 64 MiB of HBM per device.

v0:
```python
import functools
import math

import jax
import jax.numpy as jnp
import numpy as np
from jax import lax
from jax.experimental import pallas as pl
from jax.experimental.pallas import tpu as pltpu
from jax.sharding import PartitionSpec as P


def tables(count, nrows, ncols):
    left = lax.iota(jnp.int32, nrows)[:, None]
    right = lax.iota(jnp.int32, ncols)[None, :]
    phase = (left * right % count).astype(jnp.float32) * (2.0 * math.pi / count)
    return (jnp.cos(phase).astype(jnp.bfloat16), jnp.sin(phase).astype(jnp.bfloat16))


def spectral_filter(row_ids, col_ids, nrows, ncols, defocus_value, noise):
    freq_y = ((row_ids + nrows // 2) % nrows - nrows // 2).astype(jnp.float32) / nrows
    freq_x = ((col_ids + ncols // 2) % ncols - ncols // 2).astype(jnp.float32) / ncols
    radius = freq_y[:, None] ** 2 + freq_x[None, :] ** 2
    chi = math.pi * defocus_value * radius
    return -(0.9975 * jnp.sin(chi) + 0.07 * jnp.cos(chi)) * lax.rsqrt(noise)


def mm(a, b):
    return jnp.dot(a, b, preferred_element_type=jnp.float32)


def general(micrograph, bank, orient_index, noise_power, defocus):
    slab, ncols = micrograph.shape
    n_rows = lax.axis_size("rows")
    nrows = slab * n_rows
    row_pos = lax.axis_index("rows")
    lcos, lsin = tables(nrows, nrows, nrows)
    ccos, csin = tables(ncols, ncols, ncols)
    piece = lax.all_gather(micrograph, "rows", axis=0, tiled=True)
    part_re = mm(piece, ccos.T).astype(jnp.bfloat16)
    part_im = (-mm(piece, csin.T)).astype(jnp.bfloat16)
    new_re = mm(lcos, part_re) + mm(lsin, part_im)
    new_im = mm(lcos, part_im) - mm(lsin, part_re)
    chosen = jnp.take(bank, orient_index, axis=0)
    mine = lax.all_to_all(chosen, "rows", split_axis=0, concat_axis=1, tiled=True)
    filt = spectral_filter(
        lax.iota(jnp.int32, nrows),
        lax.iota(jnp.int32, ncols),
        nrows,
        ncols,
        defocus[0],
        noise_power,
    )
    scale = 1.0 / (nrows * ncols)
    tcos = ccos.T
    tsin = csin.T

    def correlate(carry, proj):
        tmp_re = mm(proj, tcos).astype(jnp.bfloat16)
        tmp_im = (-mm(proj, tsin)).astype(jnp.bfloat16)
        proj_re = mm(lcos, tmp_re) + mm(lsin, tmp_im)
        proj_im = mm(lcos, tmp_im) - mm(lsin, tmp_re)
        cross_re = (filt * (new_re * proj_re + new_im * proj_im)).astype(jnp.bfloat16)
        cross_im = (filt * (new_im * proj_re - new_re * proj_im)).astype(jnp.bfloat16)
        half_re = (mm(lcos, cross_re) - mm(lsin, cross_im)).astype(jnp.bfloat16)
        half_im = (mm(lcos, cross_im) + mm(lsin, cross_re)).astype(jnp.bfloat16)
        corr = (mm(half_re, ccos) - mm(half_im, csin)) * scale
        best_now, sum_now, square_now = carry
        return ((jnp.maximum(best_now, corr), sum_now + corr, square_now + corr * corr), None)

    start = (
        jnp.full((nrows, ncols), -jnp.inf, jnp.float32),
        jnp.zeros((nrows, ncols), jnp.float32),
        jnp.zeros((nrows, ncols), jnp.float32),
    )
    (best, summed, squared), _ = lax.scan(correlate, start, mine)
    width = ncols // lax.axis_size("orient")
    best = lax.pmax(best, ("orient", "rows"))
    summed, squared = lax.psum((summed, squared), ("orient", "rows"))
    first_col = lax.axis_index("orient") * width
    first_row = row_pos * slab

    def block(field):
        picked = lax.dynamic_slice_in_dim(field, first_row, slab, 0)
        return lax.dynamic_slice_in_dim(picked, first_col, width, 1)

    peak = block(best)
    total = block(summed)
    squares = block(squared)
    return (peak, total, squares)

MESH = pl.DeviceIdType.MESH


def wide_table(count):
    index = np.arange(count)
    phase = (index[:, None] * index[None, :] % count).astype(np.float32) * np.float32(2.0 * math.pi / count)
    cos = np.cos(phase)
    sin = np.sin(phase)
    return np.concatenate([sin, cos, -sin], axis=1).astype(jnp.bfloat16)


def dot(a, b):
    return jnp.dot(a, b, preferred_element_type=jnp.float32)


def kernel(n, m, size, defocus, mic, chosen, noise_hbm, table_hbm, peak, total, squares,
           noise, table, mics, projs, tmp, spec_re, spec_im, cross, half, stage, inbox,
           local_sem, mic_send, mic_recv, bank_send, bank_recv, out_send, out_recv):
    row = lax.axis_index("rows")
    col = lax.axis_index("orient")
    slab = size // n
    width = size // m
    me = row * m + col
    barrier = pltpu.get_barrier_semaphore()
    for a in range(n):
        for b in range(m):
            if a or b:
                peer = {"rows": lax.rem(row + a, n), "orient": lax.rem(col + b, m)}
                pl.semaphore_signal(barrier, inc=1, device_id=peer, device_id_type=MESH)
    table_copy = pltpu.make_async_copy(table_hbm, table, local_sem.at[0])
    noise_copy = pltpu.make_async_copy(noise_hbm, noise, local_sem.at[1])
    table_copy.start()
    noise_copy.start()
    pl.semaphore_wait(barrier, n * m - 1)

    order = sorted(range(1, n), key=lambda s: (s != n // 2, s))

    def mic_copy(peer, slot):
        return pltpu.make_async_remote_copy(
            src_ref=mic, dst_ref=mics.at[slot], send_sem=mic_send.at[peer], recv_sem=mic_recv.at[slot],
            device_id={"rows": peer}, device_id_type=MESH)

    def bank_copy(peer, slot):
        return pltpu.make_async_remote_copy(
            src_ref=chosen.at[peer], dst_ref=projs.at[slot], send_sem=bank_send.at[peer], recv_sem=bank_recv.at[slot],
            device_id={"rows": peer}, device_id_type=MESH)

    for s in order:
        mic_copy(lax.rem(row + s, n), row).start()
    for s in order:
        bank_copy(lax.rem(row + s, n), row).start()

    def row_dft(block, source):
        at = pl.multiple_of(source * slab, slab)
        both = dot(block, table[:, 0:2 * size]).astype(jnp.bfloat16)
        tmp[pl.ds(at, slab), :] = both[:, size:]
        tmp[pl.ds(pl.multiple_of(size + source * slab, slab), slab), :] = both[:, :size]

    table_copy.wait()
    row_dft(mic[...], row)
    noise_copy.wait()
    for s in order:
        source = lax.rem(row + n - s, n)
        mic_copy(source, source).wait_recv()
        row_dft(mics[source], source)

    def freq_angle(shape, dim):
        k = lax.broadcasted_iota(jnp.int32, shape, dim)
        f = jnp.where(k < size // 2, k, k - size).astype(jnp.float32) / size
        return math.pi * defocus[0] * f * f

    step = 256
    across = freq_angle((8, size), 1)
    sin_x = jnp.sin(across)[0:1]
    cos_x = jnp.cos(across)[0:1]
    left_x = -(0.9975 * cos_x - 0.07 * sin_x)
    right_x = -(0.9975 * sin_x + 0.07 * cos_x)
    down = freq_angle((size, 128), 0)
    sin_y = jnp.sin(down)[:, 0:1]
    cos_y = jnp.cos(down)[:, 0:1]
    for g in range(size // step):
        rows_g = slice(g * step, (g + 1) * step)
        filt = (sin_y[rows_g] * left_x + cos_y[rows_g] * right_x) * lax.rsqrt(noise[rows_g, :])
        spec_re[rows_g, :] = filt * dot(table[rows_g, size:], tmp[...])
        spec_im[rows_g, :] = filt * dot(table[rows_g, :2 * size], tmp[...])

    row_dft(chosen[row], row)
    for s in order:
        source = lax.rem(row + n - s, n)
        bank_copy(source, source).wait_recv()
        row_dft(projs[source], source)
    for g in range(size // step):
        rows_g = slice(g * step, (g + 1) * step)
        p_re = dot(table[rows_g, size:], tmp[...])
        p_im = dot(table[rows_g, :2 * size], tmp[...])
        s_re = spec_re[rows_g, :]
        s_im = spec_im[rows_g, :]
        cross[rows_g, :] = (s_re * p_re + s_im * p_im).astype(jnp.bfloat16)
        cross[size + g * step:size + (g + 1) * step, :] = (s_re * p_im - s_im * p_re).astype(jnp.bfloat16)

    def out_copy(a, b, slot):
        peer = a * m + b
        return pltpu.make_async_remote_copy(
            src_ref=stage.at[peer], dst_ref=inbox.at[slot], send_sem=out_send.at[peer], recv_sem=out_recv.at[slot],
            device_id={"rows": a, "orient": b}, device_id_type=MESH)

    scale = 1.0 / (size * size)
    pairs = n // 2
    for t in range(1, pairs + 1):
        g = lax.rem(row // 2 + t, pairs)
        at = pl.ds(pl.multiple_of(g * 2 * slab, 2 * slab), 2 * slab)
        half[:, :size] = dot(table[at, size:], cross[...]).astype(jnp.bfloat16)
        half[:, size:] = dot(table[at, :2 * size], cross[...]).astype(jnp.bfloat16)
        corr = (dot(half[:, :size], table[:, size:2 * size]) + dot(half[:, size:], table[:, 2 * size:])) * scale
        corr = corr.astype(jnp.bfloat16)
        for i in range(2):
            for b in range(m):
                stage[(g * 2 + i) * m + b] = corr[i * slab:(i + 1) * slab, b * width:(b + 1) * width]
        mate = lax.rem(row, 2)
        for i in range(2):
            a = g * 2 + lax.rem(mate + 1 + i, 2)
            for s in (m // 2, *(s for s in range(m) if s != m // 2)):
                if t == pairs and i == 1 and s == 0:
                    continue
                out_copy(a, lax.rem(col + s, m), me).start()

    best = summed = stage[me].astype(jnp.float32)
    squared = best * best
    for a in range(n):
        for b in range(m):
            if a or b:
                ra = lax.rem(row + n - a, n)
                rb = lax.rem(col + m - b, m)
                source = ra * m + rb
                out_copy(ra, rb, source).wait_recv()
                value = inbox[source].astype(jnp.float32)
                best = jnp.maximum(best, value)
                summed = summed + value
                squared = squared + value * value
    peak[...] = best
    total[...] = summed
    squares[...] = squared
    for s in order:
        peer = lax.rem(row + s, n)
        mic_copy(peer, row).wait_send()
        bank_copy(peer, row).wait_send()
    for a in range(n):
        for b in range(m):
            if a or b:
                out_copy(lax.rem(row + a, n), lax.rem(col + b, m), me).wait_send()


def local(micrograph, bank, orient_index, noise_power, defocus):
    slab, size = micrograph.shape
    n = lax.axis_size("rows")
    m = lax.axis_size("orient")
    fits = size == slab * n and n % 2 == 0 and slab % 128 == 0 and (size // m) % 128 == 0 and size % 256 == 0
    if not (fits and orient_index.shape[0] == n):
        return general(micrograph, bank, orient_index, noise_power, defocus)
    chosen = jnp.take(bank, orient_index, axis=0)
    table = jnp.asarray(wide_table(size))
    width = size // m
    out = jax.ShapeDtypeStruct((slab, width), jnp.float32)
    vmem = pl.BlockSpec(memory_space=pltpu.VMEM)
    hbm = pl.BlockSpec(memory_space=pl.ANY)
    bf16 = jnp.bfloat16
    dma = pltpu.SemaphoreType.DMA
    return pl.pallas_call(
        functools.partial(kernel, n, m, size),
        out_shape=(out, out, out),
        in_specs=[pl.BlockSpec(memory_space=pltpu.SMEM), vmem, vmem, hbm, hbm],
        out_specs=(vmem, vmem, vmem),
        scratch_shapes=[
            pltpu.VMEM((size, size), jnp.float32),
            pltpu.VMEM((size, 3 * size), bf16),
            pltpu.VMEM((n, slab, size), bf16),
            pltpu.VMEM((n, slab, size), bf16),
            pltpu.VMEM((2 * size, size), bf16),
            pltpu.VMEM((size, size), jnp.float32),
            pltpu.VMEM((size, size), jnp.float32),
            pltpu.VMEM((2 * size, size), bf16),
            pltpu.VMEM((2 * slab, 2 * size), bf16),
            pltpu.VMEM((n * m, slab, width), bf16),
            pltpu.VMEM((n * m, slab, width), bf16),
            dma((2,)), dma((n,)), dma((n,)), dma((n,)), dma((n,)), dma((n * m,)), dma((n * m,)),
        ],
        compiler_params=pltpu.CompilerParams(collective_id=0, has_side_effects=True, vmem_limit_bytes=48 * 1024 * 1024),
        name="correlate",
    )(defocus, micrograph, chosen, noise_power, table)


def solution(mesh):
    in_specs = (
        P(("grp", "rows"), None),
        P(None, "rows", None),
        P("orient"),
        P("grp", None),
        P("grp"),
    )
    out_specs = (
        P(("grp", "rows"), "orient"),
        P(("grp", "rows"), "orient"),
        P(("grp", "rows"), "orient"),
    )
    return jax.shard_map(local, mesh=mesh, in_specs=in_specs, out_specs=out_specs, check_vma=False)
```

profile of v0, /device:TPU:0, one launch (start us, length us, event | category | flops | bytes accessed | tf_op | source)
XLA Modules:
  0.0 42.8 jit_solution(11837244319237718631)
XLA Ops:
  0.6 0.0 copy-start
  1.4 0.7 %compare_and_fusion = pred[4]{0:T(512)(128)(4,1)S(1)} fusion(s32[4]{0:T(128)} %param.8), kind=kLoop, calls=%fused_computation.4 | loop fusion | flops 24 | bytes 20 | tf_op jit(solution)/shard_map/jit(_take)/and | solution.py:251
  2.1 0.7 %compare_select_fusion = s32[4]{0:T(128)S(1)} fusion(s32[4]{0:T(128)} %param.8), kind=kLoop, calls=%fused_computation.3 | loop fusion | flops 12 | bytes 32 | tf_op jit(solution)/shard_map/jit(_take)/jit(_where)/select_n | solution.py:251
  2.8 0.0 copy-done
  2.8 0.6 %gather_fusion = bf16[4,128,512]{2,1,0:T(8,128)(2,1)S(1)} fusion(bf16[20,128,512]{2,1,0:T(8,128)(2,1)S(1)} %copy-done, s32[1024]{0:T(1024)S(1)} %pad_clamp_fusion), kind=kCustom, calls=%fused_computation | custom fusion | bytes 1048592 | tf_op jit(solution)/shard_map/jit(_take)/gather | solution.py:251
  3.4 0.1 broadcast_select_fusion.chosen
  3.5 0.0 copy-start.1
  3.5 1.4 %copy-done.1 = bf16[512,1536]{1,0:T(8,128)(2,1)S(1)} copy-done((bf16[512,1536]{1,0:T(8,128)(2,1)S(1)}, bf16[512,1536]{1,0:T(8,128)(2,1)}, u32[]{:S(2)}) %copy-start.1) | copy-done | bytes 1572888
  4.9 0.0 copy-start.2
  4.9 1.2 %copy-done.2 = f32[512,512]{1,0:T(8,128)S(1)} copy-done((f32[512,512]{1,0:T(8,128)S(1)}, f32[512,512]{1,0:T(8,128)}, u32[]{:S(2)}) %copy-start.2) | copy-done | bytes 1048600
  6.1 0.0 copy-start.3
  6.1 0.9 %copy-done.3 = bf16[128,512]{1,0:T(8,128)(2,1)S(1)} copy-done((bf16[128,512]{1,0:T(8,128)(2,1)S(1)}, bf16[128,512]{1,0:T(8,128)(2,1)}, u32[]{:S(2)}) %copy-start.3) | copy-done | bytes 131096
  7.0 33.9 %correlate.1 = (f32[128,128]{1,0:T(8,128)S(1)}, f32[128,128]{1,0:T(8,128)S(1)}, f32[128,128]{1,0:T(8,128)S(1)}) custom-call(f32[1]{0:T(128)S(6)} %copy.12.defocus, bf16[128,512]{1,0:T(8,128)(2,1)S(1)} %copy-done.3, bf16[4,128,512]{2,1,0:T(8,128)(2,1)S(1)} %broadcast_select_fusion.chosen, f32[512,512]{1,0:T(8,128)S(1)} %copy-done.2, ...), custom_call_target="tpu_custom_call" | custom-call | tf_op jit(solution)/shard_map/correlate/pallas_call | solution.py:259
  40.9 0.6 %copy.13 = f32[128,128]{1,0:T(8,128)} copy(f32[128,128]{1,0:T(8,128)S(1)} %get-tuple-element.6) | data formatting | bytes 131072
  41.5 0.6 %copy.14 = f32[128,128]{1,0:T(8,128)} copy(f32[128,128]{1,0:T(8,128)S(1)} %get-tuple-element.7) | data formatting | bytes 131072
  42.2 0.6 %copy.15 = f32[128,128]{1,0:T(8,128)} copy(f32[128,128]{1,0:T(8,128)S(1)} %get-tuple-element.8) | data formatting | bytes 131072
  (1 shorter events, 0.0 us)
Async XLA Ops:
  0.6 2.1 %copy-start = (bf16[20,128,512]{2,1,0:T(8,128)(2,1)S(1)}, bf16[20,128,512]{2,1,0:T(8,128)(2,1)}, u32[]{:S(2)}) copy-start(bf16[20,128,512]{2,1,0:T(8,128)(2,1)} %param.7) | copy-start | bytes 7864324
  3.5 1.4 %copy-start.1 = (bf16[512,1536]{1,0:T(8,128)(2,1)S(1)}, bf16[512,1536]{1,0:T(8,128)(2,1)}, u32[]{:S(2)}) copy-start(bf16[512,1536]{1,0:T(8,128)(2,1)} %constant.18.clone.table_hbm) | copy-start | bytes 4718596
  4.9 1.2 %copy-start.2 = (f32[512,512]{1,0:T(8,128)S(1)}, f32[512,512]{1,0:T(8,128)}, u32[]{:S(2)}) copy-start(f32[512,512]{1,0:T(8,128)} %noise_hbm.1) | copy-start | bytes 3145732
  6.1 0.9 %copy-start.3 = (bf16[128,512]{1,0:T(8,128)(2,1)S(1)}, bf16[128,512]{1,0:T(8,128)(2,1)}, u32[]{:S(2)}) copy-start(bf16[128,512]{1,0:T(8,128)(2,1)} %mic.1) | copy-start | bytes 393220
where the time goes:
time: 43 us; the launch traced here: 42.8 us
  Pallas kernels  33.9 us (79%)
  local copies, waits for them, and re-layouts  6.01 us (14%)
  between operations  1.47 us (3%)
  other arithmetic  1.45 us (3%)
    pallas_call x1, Pallas kernels, local(): pl.pallas_call(functools.partial(kernel, n, m, size), out_shape=(out, out...  33.9 us
    unnamed x11, local copies, waits for them, and re-layouts  5.43 us

commit v1 on v0

--- a/solution.py
+++ b/solution.py
@@ -104,56 +104,77 @@
     return jnp.dot(a, b, preferred_element_type=jnp.float32)
 
 
-def kernel(n, m, size, defocus, mic, chosen, noise_hbm, table_hbm, peak, total, squares,
-           noise, table, mics, projs, tmp, spec_re, spec_im, cross, half, stage, inbox,
-           local_sem, mic_send, mic_recv, bank_send, bank_recv, out_send, out_recv):
+def kernel(n, m, size, defocus, index, mic_hbm, bank_hbm, noise_hbm, table_hbm, peak, total, squares,
+           bank, chosen, mic, noise, table, mics, halves, beside, tmp_mic, tmp, proj_re, proj_im, cross, half, stage, inbox,
+           local_sem, near, out_send, out_recv):
     row = lax.axis_index("rows")
     col = lax.axis_index("orient")
     slab = size // n
     width = size // m
     me = row * m + col
+    grp = lax.axis_index("grp")
+    over = row + 2 - 4 * (row // 2)
+    mate = row + 1 - 2 * lax.rem(row, 2)
+    corner = mate + 2 - 4 * (mate // 2)
+    piece = slab // 2
     barrier = pltpu.get_barrier_semaphore()
     for a in range(n):
         for b in range(m):
             if a or b:
                 peer = {"rows": lax.rem(row + a, n), "orient": lax.rem(col + b, m)}
                 pl.semaphore_signal(barrier, inc=1, device_id=peer, device_id_type=MESH)
-    table_copy = pltpu.make_async_copy(table_hbm, table, local_sem.at[0])
-    noise_copy = pltpu.make_async_copy(noise_hbm, noise, local_sem.at[1])
-    table_copy.start()
-    noise_copy.start()
-    pl.semaphore_wait(barrier, n * m - 1)
-
-    order = sorted(range(1, n), key=lambda s: (s != n // 2, s))
-
-    def mic_copy(peer, slot):
+    pl.semaphore_signal(barrier, inc=1, device_id={"grp": 1 - grp}, device_id_type=MESH)
+    mic_in = pltpu.make_async_copy(mic_hbm, mic, local_sem.at[0])
+    table_in = pltpu.make_async_copy(table_hbm, table, local_sem.at[1])
+    noise_in = pltpu.make_async_copy(noise_hbm, noise, local_sem.at[2])
+    bank_in = pltpu.make_async_copy(bank_hbm, bank, local_sem.at[3])
+    bank_in.start()
+    mic_in.start()
+    table_in.start()
+    noise_in.start()
+    bank_in.wait()
+    for d in range(n):
+        chosen[d] = bank[index[d]]
+    mic_in.wait()
+    pl.semaphore_wait(barrier, n * m)
+
+    def remote(src, dst, sems, at, to):
         return pltpu.make_async_remote_copy(
-            src_ref=mic, dst_ref=mics.at[slot], send_sem=mic_send.at[peer], recv_sem=mic_recv.at[slot],
-            device_id={"rows": peer}, device_id_type=MESH)
-
-    def bank_copy(peer, slot):
-        return pltpu.make_async_remote_copy(
-            src_ref=chosen.at[peer], dst_ref=projs.at[slot], send_sem=bank_send.at[peer], recv_sem=bank_recv.at[slot],
-            device_id={"rows": peer}, device_id_type=MESH)
-
-    for s in order:
-        mic_copy(lax.rem(row + s, n), row).start()
-    for s in order:
-        bank_copy(lax.rem(row + s, n), row).start()
-
-    def row_dft(block, source):
+            src_ref=src, dst_ref=dst, send_sem=sems.at[0, at], recv_sem=sems.at[1, at],
+            device_id=to, device_id_type=MESH)
+
+    bank_over = remote(chosen.at[over, pl.ds(grp * piece, piece)], halves.at[0, grp], near, 0, {"rows": over})
+    bank_corner = remote(chosen.at[corner, pl.ds(grp * piece, piece)], halves.at[1, grp], near, 1, {"rows": corner})
+    bank_mate = remote(chosen.at[mate], beside.at[0], near, 2, {"rows": mate})
+    mic_over = remote(mic, mics.at[0], near, 3, {"rows": over})
+    mic_mate = remote(mic, mics.at[1], near, 4, {"rows": mate})
+    mic_pass = remote(mics.at[0], mics.at[2], near, 5, {"rows": mate})
+    pass_over = remote(halves.at[0, grp], halves.at[0, grp], near, 6, {"grp": 1 - grp})
+    pass_corner = remote(halves.at[1, grp], halves.at[1, grp], near, 7, {"grp": 1 - grp})
+    bank_over.start()
+    bank_corner.start()
+    mic_over.start()
+    mic_mate.start()
+    bank_mate.start()
+
+    def row_dft(into, block, source):
         at = pl.multiple_of(source * slab, slab)
         both = dot(block, table[:, 0:2 * size]).astype(jnp.bfloat16)
-        tmp[pl.ds(at, slab), :] = both[:, size:]
-        tmp[pl.ds(pl.multiple_of(size + source * slab, slab), slab), :] = both[:, :size]
-
-    table_copy.wait()
-    row_dft(mic[...], row)
-    noise_copy.wait()
-    for s in order:
-        source = lax.rem(row + n - s, n)
-        mic_copy(source, source).wait_recv()
-        row_dft(mics[source], source)
+        into[pl.ds(at, slab), :] = both[:, size:]
+        into[pl.ds(pl.multiple_of(size + source * slab, slab), slab), :] = both[:, :size]
+
+    table_in.wait()
+    row_dft(tmp_mic, mic[...], row)
+    row_dft(tmp, chosen[row], row)
+    bank_over.wait_recv()
+    pass_over.start()
+    mic_mate.wait_recv()
+    row_dft(tmp_mic, mics[1], mate)
+    bank_corner.wait_recv()
+    pass_corner.start()
+    bank_mate.wait_recv()
+    row_dft(tmp, beside[0], mate)
+    noise_in.wait()
 
     def freq_angle(shape, dim):
         k = lax.broadcasted_iota(jnp.int32, shape, dim)
@@ -171,21 +192,26 @@
     cos_y = jnp.cos(down)[:, 0:1]
     for g in range(size // step):
         rows_g = slice(g * step, (g + 1) * step)
-        filt = (sin_y[rows_g] * left_x + cos_y[rows_g] * right_x) * lax.rsqrt(noise[rows_g, :])
-        spec_re[rows_g, :] = filt * dot(table[rows_g, size:], tmp[...])
-        spec_im[rows_g, :] = filt * dot(table[rows_g, :2 * size], tmp[...])
-
-    row_dft(chosen[row], row)
-    for s in order:
-        source = lax.rem(row + n - s, n)
-        bank_copy(source, source).wait_recv()
-        row_dft(projs[source], source)
+        noise[rows_g, :] = (sin_y[rows_g] * left_x + cos_y[rows_g] * right_x) * lax.rsqrt(noise[rows_g, :])
+    pass_over.wait_recv()
+    row_dft(tmp, halves[0].reshape(slab, size), over)
+    mic_over.wait_recv()
+    mic_pass.start()
+    pass_corner.wait_recv()
+    row_dft(tmp, halves[1].reshape(slab, size), corner)
+    row_dft(tmp_mic, mics[0], over)
     for g in range(size // step):
         rows_g = slice(g * step, (g + 1) * step)
-        p_re = dot(table[rows_g, size:], tmp[...])
-        p_im = dot(table[rows_g, :2 * size], tmp[...])
-        s_re = spec_re[rows_g, :]
-        s_im = spec_im[rows_g, :]
+        proj_re[rows_g, :] = noise[rows_g, :] * dot(table[rows_g, size:], tmp[...])
+        proj_im[rows_g, :] = noise[rows_g, :] * dot(table[rows_g, :2 * size], tmp[...])
+    mic_pass.wait_recv()
+    row_dft(tmp_mic, mics[2], corner)
+    for g in range(size // step):
+        rows_g = slice(g * step, (g + 1) * step)
+        s_re = dot(table[rows_g, size:], tmp_mic[...])
+        s_im = dot(table[rows_g, :2 * size], tmp_mic[...])
+        p_re = proj_re[rows_g, :]
+        p_im = proj_im[rows_g, :]
         cross[rows_g, :] = (s_re * p_re + s_im * p_im).astype(jnp.bfloat16)
         cross[size + g * step:size + (g + 1) * step, :] = (s_re * p_im - s_im * p_re).astype(jnp.bfloat16)
 
@@ -207,9 +233,8 @@
         for i in range(2):
             for b in range(m):
                 stage[(g * 2 + i) * m + b] = corr[i * slab:(i + 1) * slab, b * width:(b + 1) * width]
-        mate = lax.rem(row, 2)
         for i in range(2):
-            a = g * 2 + lax.rem(mate + 1 + i, 2)
+            a = g * 2 + lax.rem(row + 1 + i, 2)
             for s in (m // 2, *(s for s in range(m) if s != m // 2)):
                 if t == pairs and i == 1 and s == 0:
                     continue
@@ -231,41 +256,50 @@
     peak[...] = best
     total[...] = summed
     squares[...] = squared
-    for s in order:
-        peer = lax.rem(row + s, n)
-        mic_copy(peer, row).wait_send()
-        bank_copy(peer, row).wait_send()
+    for copy in (bank_over, bank_corner, bank_mate, mic_over, mic_mate, mic_pass, pass_over, pass_corner):
+        copy.wait_send()
     for a in range(n):
         for b in range(m):
             if a or b:
                 out_copy(lax.rem(row + a, n), lax.rem(col + b, m), me).wait_send()
 
 
+def write_out(peak_in, total_in, squares_in, peak, total, squares):
+    peak[...] = peak_in[...]
+    total[...] = total_in[...]
+    squares[...] = squares_in[...]
+
+
 def local(micrograph, bank, orient_index, noise_power, defocus):
     slab, size = micrograph.shape
     n = lax.axis_size("rows")
     m = lax.axis_size("orient")
-    fits = size == slab * n and n % 2 == 0 and slab % 128 == 0 and (size // m) % 128 == 0 and size % 256 == 0
-    if not (fits and orient_index.shape[0] == n):
+    fits = size == slab * n and n == 4 and lax.axis_size("grp") == 2 and slab % 128 == 0 and (size // m) % 128 == 0 and size % 256 == 0
+    if not (fits and orient_index.shape[0] == n and bank.shape[0] <= 64):
         return general(micrograph, bank, orient_index, noise_power, defocus)
-    chosen = jnp.take(bank, orient_index, axis=0)
     table = jnp.asarray(wide_table(size))
     width = size // m
     out = jax.ShapeDtypeStruct((slab, width), jnp.float32)
     vmem = pl.BlockSpec(memory_space=pltpu.VMEM)
     hbm = pl.BlockSpec(memory_space=pl.ANY)
+    smem = pl.BlockSpec(memory_space=pltpu.SMEM)
     bf16 = jnp.bfloat16
     dma = pltpu.SemaphoreType.DMA
-    return pl.pallas_call(
+    maps = pl.pallas_call(
         functools.partial(kernel, n, m, size),
         out_shape=(out, out, out),
-        in_specs=[pl.BlockSpec(memory_space=pltpu.SMEM), vmem, vmem, hbm, hbm],
+        in_specs=[smem, smem, hbm, hbm, hbm, hbm],
         out_specs=(vmem, vmem, vmem),
         scratch_shapes=[
+            pltpu.VMEM(bank.shape, bf16),
+            pltpu.VMEM((n, slab, size), bf16),
+            pltpu.VMEM((slab, size), bf16),
             pltpu.VMEM((size, size), jnp.float32),
             pltpu.VMEM((size, 3 * size), bf16),
-            pltpu.VMEM((n, slab, size), bf16),
-            pltpu.VMEM((n, slab, size), bf16),
+            pltpu.VMEM((3, slab, size), bf16),
+            pltpu.VMEM((2, 2, slab // 2, size), bf16),
+            pltpu.VMEM((1, slab, size), bf16),
+            pltpu.VMEM((2 * size, size), bf16),
             pltpu.VMEM((2 * size, size), bf16),
             pltpu.VMEM((size, size), jnp.float32),
             pltpu.VMEM((size, size), jnp.float32),
@@ -273,11 +307,18 @@
             pltpu.VMEM((2 * slab, 2 * size), bf16),
             pltpu.VMEM((n * m, slab, width), bf16),
             pltpu.VMEM((n * m, slab, width), bf16),
-            dma((2,)), dma((n,)), dma((n,)), dma((n,)), dma((n,)), dma((n * m,)), dma((n * m,)),
+            dma((4,)), dma((2, 8)), dma((n * m,)), dma((n * m,)),
         ],
-        compiler_params=pltpu.CompilerParams(collective_id=0, has_side_effects=True, vmem_limit_bytes=48 * 1024 * 1024),
+        compiler_params=pltpu.CompilerParams(collective_id=0, has_side_effects=True, vmem_limit_bytes=60 * 1024 * 1024),
         name="correlate",
-    )(defocus, micrograph, chosen, noise_power, table)
+    )(defocus, orient_index, micrograph, bank, noise_power, table)
+    return pl.pallas_call(
+        write_out,
+        out_shape=(out, out, out),
+        in_specs=[vmem] * 3,
+        out_specs=(vmem, vmem, vmem),
+        name="write_out",
+    )(*maps)
 
 
 def solution(mesh):

time: 43 us -> 36.6 us (0.85)
  local copies, waits for them, and re-layouts: 6.01 us -> 0 us
  other arithmetic: 1.45 us -> 0 us
  Pallas kernels: 33.9 us -> 35.1 us
    unnamed x11 -> x0, local copies, waits for them, and re-layouts: 5.43 us -> none
    pallas_call x0 -> x1, Pallas kernels: none -> 1.58 us  [local(): pl.pallas_call(write_out, out_shape=(out, out, out), in_specs=[vmem] * 3,...]
    select_n x2 -> x0, other arithmetic: 0.77 us -> none  [local(): chosen = jnp.take(bank, orient_index, axis=0)]
    and x1 -> x0, other arithmetic: 0.66 us -> none  [local(): chosen = jnp.take(bank, orient_index, axis=0)]
    gather x1 -> x0, local copies, waits for them, and re-layouts: 0.58 us -> none  [local(): chosen = jnp.take(bank, orient_index, axis=0)]
where the time goes in v1:
time: 36.6 us; the launch traced here: 36.4 us
  Pallas kernels  35.1 us (96%)
  between operations  1.29 us (4%)
    pallas_call x1, Pallas kernels, local(): pl.pallas_call(functools.partial(kernel, n, m, size), out_shape=(out, out...  33.5 us
    pallas_call x1, Pallas kernels, local(): pl.pallas_call(write_out, out_shape=(out, out, out), in_specs=[vmem] * 3,...  1.58 us

profile of v1, /device:TPU:0, one launch (start us, length us, event | category | flops | bytes accessed | tf_op | source)
XLA Modules:
  0.0 36.4 jit_solution(16925085088434863195)
XLA Ops:
  1.3 33.5 %correlate.1 = (f32[128,128]{1,0:T(8,128)}, f32[128,128]{1,0:T(8,128)}, f32[128,128]{1,0:T(8,128)}) custom-call(f32[1]{0:T(128)S(6)} %copy.9.defocus, s32[4]{0:T(128)} %index.1, bf16[128,512]{1,0:T(8,128)(2,1)} %mic_hbm.1, bf16[20,128,512]{2,1,0:T(8,128)(2,1)} %bank_hbm.1, f32[512,512]{1,0:T(8,128)} %noise_hbm.1, bf16[512,1536]{1,0:T(8,128)(2,1)} %constant.2.clone.table_hbm), custom_call_target="tpu_custom_call" | custom-call | tf_op jit(solution)/shard_map/correlate/pallas_call | solution.py:288
  34.8 1.6 %write_out.1 = (f32[128,128]{1,0:T(8,128)}, f32[128,128]{1,0:T(8,128)}, f32[128,128]{1,0:T(8,128)}) custom-call(f32[128,128]{1,0:T(8,128)} %get-tuple-element.6.peak_in, f32[128,128]{1,0:T(8,128)} %get-tuple-element.7.total_in, f32[128,128]{1,0:T(8,128)} %get-tuple-element.8.squares_in), custom_call_target="tpu_custom_call" | custom-call | tf_op jit(solution)/shard_map/write_out/pallas_call | solution.py:315

commit v2 on v1

--- a/solution.py
+++ b/solution.py
@@ -105,24 +105,28 @@
 
 
 def kernel(n, m, size, defocus, index, mic_hbm, bank_hbm, noise_hbm, table_hbm, peak, total, squares,
-           bank, chosen, mic, noise, table, mics, halves, beside, tmp_mic, tmp, proj_re, proj_im, cross, half, stage, inbox,
+           bank, chosen, mic, noise, table, mics, halves, beside, tmp_mic, tmp, proj_re, proj_im, cross, half, stage, inbox, part,
            local_sem, near, out_send, out_recv):
     row = lax.axis_index("rows")
     col = lax.axis_index("orient")
     slab = size // n
     width = size // m
-    me = row * m + col
+    me = row * 2 + lax.rem(col, 2)
     grp = lax.axis_index("grp")
     over = row + 2 - 4 * (row // 2)
     mate = row + 1 - 2 * lax.rem(row, 2)
     corner = mate + 2 - 4 * (mate // 2)
     piece = slab // 2
     barrier = pltpu.get_barrier_semaphore()
+    low = 2 * (col // 2)
+    far = 2 - low
     for a in range(n):
-        for b in range(m):
+        for b in range(2):
             if a or b:
-                peer = {"rows": lax.rem(row + a, n), "orient": lax.rem(col + b, m)}
+                peer = {"rows": lax.rem(row + a, n), "orient": low + lax.rem(col + b, 2)}
                 pl.semaphore_signal(barrier, inc=1, device_id=peer, device_id_type=MESH)
+    twin = {"orient": far + lax.rem(col, 2)}
+    pl.semaphore_signal(barrier, inc=1, device_id=twin, device_id_type=MESH)
     pl.semaphore_signal(barrier, inc=1, device_id={"grp": 1 - grp}, device_id_type=MESH)
     mic_in = pltpu.make_async_copy(mic_hbm, mic, local_sem.at[0])
     table_in = pltpu.make_async_copy(table_hbm, table, local_sem.at[1])
@@ -136,7 +140,7 @@
     for d in range(n):
         chosen[d] = bank[index[d]]
     mic_in.wait()
-    pl.semaphore_wait(barrier, n * m)
+    pl.semaphore_wait(barrier, 2 * n + 1)
 
     def remote(src, dst, sems, at, to):
         return pltpu.make_async_remote_copy(
@@ -215,53 +219,80 @@
         cross[rows_g, :] = (s_re * p_re + s_im * p_im).astype(jnp.bfloat16)
         cross[size + g * step:size + (g + 1) * step, :] = (s_re * p_im - s_im * p_re).astype(jnp.bfloat16)
 
-    def out_copy(a, b, slot):
-        peer = a * m + b
+    def out_copy(kind, a, b, slot):
+        peer = a * 2 + b
         return pltpu.make_async_remote_copy(
-            src_ref=stage.at[peer], dst_ref=inbox.at[slot], send_sem=out_send.at[peer], recv_sem=out_recv.at[slot],
-            device_id={"rows": a, "orient": b}, device_id_type=MESH)
+            src_ref=stage.at[kind, peer], dst_ref=inbox.at[kind, slot],
+            send_sem=out_send.at[kind, peer], recv_sem=out_recv.at[kind, slot],
+            device_id={"rows": a, "orient": low + b}, device_id_type=MESH)
 
     scale = 1.0 / (size * size)
     pairs = n // 2
-    for t in range(1, pairs + 1):
+    side = lax.rem(col, 2)
+
+    def send_blocks(kind, t):
         g = lax.rem(row // 2 + t, pairs)
-        at = pl.ds(pl.multiple_of(g * 2 * slab, 2 * slab), 2 * slab)
-        half[:, :size] = dot(table[at, size:], cross[...]).astype(jnp.bfloat16)
-        half[:, size:] = dot(table[at, :2 * size], cross[...]).astype(jnp.bfloat16)
-        corr = (dot(half[:, :size], table[:, size:2 * size]) + dot(half[:, size:], table[:, 2 * size:])) * scale
+        begin = (far if kind == 0 else low) * width
+        cos_at = pl.ds(pl.multiple_of(size + begin, 2 * width), 2 * width)
+        sin_at = pl.ds(pl.multiple_of(2 * size + begin, 2 * width), 2 * width)
+        corr = (dot(half[t - 1, :, :size], table[:, cos_at]) + dot(half[t - 1, :, size:], table[:, sin_at])) * scale
         corr = corr.astype(jnp.bfloat16)
         for i in range(2):
-            for b in range(m):
-                stage[(g * 2 + i) * m + b] = corr[i * slab:(i + 1) * slab, b * width:(b + 1) * width]
+            for b in range(2):
+                stage[kind, (g * 2 + i) * 2 + b] = corr[i * slab:(i + 1) * slab, b * width:(b + 1) * width]
         for i in range(2):
             a = g * 2 + lax.rem(row + 1 + i, 2)
-            for s in (m // 2, *(s for s in range(m) if s != m // 2)):
+            for s in (1, 0):
                 if t == pairs and i == 1 and s == 0:
                     continue
-                out_copy(a, lax.rem(col + s, m), me).start()
-
-    best = summed = stage[me].astype(jnp.float32)
-    squared = best * best
-    for a in range(n):
-        for b in range(m):
-            if a or b:
-                ra = lax.rem(row + n - a, n)
-                rb = lax.rem(col + m - b, m)
-                source = ra * m + rb
-                out_copy(ra, rb, source).wait_recv()
-                value = inbox[source].astype(jnp.float32)
-                best = jnp.maximum(best, value)
-                summed = summed + value
-                squared = squared + value * value
+                out_copy(kind, a, lax.rem(side + s, 2), me).start()
+
+    for t in range(1, pairs + 1):
+        at = pl.ds(pl.multiple_of(lax.rem(row // 2 + t, pairs) * 2 * slab, 2 * slab), 2 * slab)
+        half[t - 1, :, :size] = dot(table[at, size:], cross[...]).astype(jnp.bfloat16)
+        half[t - 1, :, size:] = dot(table[at, :2 * size], cross[...]).astype(jnp.bfloat16)
+        send_blocks(0, t)
+    for t in range(1, pairs + 1):
+        send_blocks(1, t)
+
+    def combine(kind):
+        best = summed = stage[kind, me].astype(jnp.float32)
+        squared = best * best
+        for a in range(n):
+            for b in range(2):
+                if a or b:
+                    ra = lax.rem(row + n - a, n)
+                    rb = lax.rem(side + b, 2)
+                    source = ra * 2 + rb
+                    out_copy(kind, ra, rb, source).wait_recv()
+                    value = inbox[kind, source].astype(jnp.float32)
+                    best = jnp.maximum(best, value)
+                    summed = summed + value
+                    squared = squared + value * value
+        return best, summed, squared
+
+    best, summed, squared = combine(0)
+    part[0, 0] = best.astype(jnp.bfloat16)
+    part[0, 1] = summed.astype(jnp.bfloat16)
+    part[0, 2] = squared.astype(jnp.bfloat16)
+    part_copy = remote(part.at[0], part.at[1], near, 8, twin)
+    part_copy.start()
+    best, summed, squared = combine(1)
+    part_copy.wait_recv()
+    best = jnp.maximum(best, part[1, 0].astype(jnp.float32))
+    summed = summed + part[1, 1].astype(jnp.float32)
+    squared = squared + part[1, 2].astype(jnp.float32)
     peak[...] = best
     total[...] = summed
     squares[...] = squared
     for copy in (bank_over, bank_corner, bank_mate, mic_over, mic_mate, mic_pass, pass_over, pass_corner):
         copy.wait_send()
-    for a in range(n):
-        for b in range(m):
-            if a or b:
-                out_copy(lax.rem(row + a, n), lax.rem(col + b, m), me).wait_send()
+    part_copy.wait_send()
+    for kind in range(2):
+        for a in range(n):
+            for b in range(2):
+                if a or b:
+                    out_copy(kind, lax.rem(row + a, n), lax.rem(side + b, 2), me).wait_send()
 
 
 def write_out(peak_in, total_in, squares_in, peak, total, squares):
@@ -274,7 +305,7 @@
     slab, size = micrograph.shape
     n = lax.axis_size("rows")
     m = lax.axis_size("orient")
-    fits = size == slab * n and n == 4 and lax.axis_size("grp") == 2 and slab % 128 == 0 and (size // m) % 128 == 0 and size % 256 == 0
+    fits = size == slab * n and n == 4 and m == 4 and lax.axis_size("grp") == 2 and slab % 128 == 0 and (size // m) % 128 == 0 and size % 256 == 0
     if not (fits and orient_index.shape[0] == n and bank.shape[0] <= 64):
         return general(micrograph, bank, orient_index, noise_power, defocus)
     table = jnp.asarray(wide_table(size))
@@ -304,10 +335,11 @@
             pltpu.VMEM((size, size), jnp.float32),
             pltpu.VMEM((size, size), jnp.float32),
             pltpu.VMEM((2 * size, size), bf16),
-            pltpu.VMEM((2 * slab, 2 * size), bf16),
-            pltpu.VMEM((n * m, slab, width), bf16),
-            pltpu.VMEM((n * m, slab, width), bf16),
-            dma((4,)), dma((2, 8)), dma((n * m,)), dma((n * m,)),
+            pltpu.VMEM((n // 2, 2 * slab, 2 * size), bf16),
+            pltpu.VMEM((2, 2 * n, slab, width), bf16),
+            pltpu.VMEM((2, 2 * n, slab, width), bf16),
+            pltpu.VMEM((2, 3, slab, width), bf16),
+            dma((4,)), dma((2, 9)), dma((2, 2 * n)), dma((2, 2 * n)),
         ],
         compiler_params=pltpu.CompilerParams(collective_id=0, has_side_effects=True, vmem_limit_bytes=60 * 1024 * 1024),
         name="correlate",

time: 36.6 us -> 35 us (0.956)
  Pallas kernels: 35.1 us -> 33.6 us
    pallas_call x1, Pallas kernels: 33.5 us -> 32 us  [local(): pl.pallas_call(functools.partial(kernel, n, m, size), out_shape=(out, out...]
where the time goes in v2:
time: 35 us; the launch traced here: 34.8 us
  Pallas kernels  33.6 us (96%)
  between operations  1.29 us (4%)
    pallas_call x1, Pallas kernels, local(): pl.pallas_call(functools.partial(kernel, n, m, size), out_shape=(out, out...  32 us
    pallas_call x1, Pallas kernels, local(): pl.pallas_call(write_out, out_shape=(out, out, out), in_specs=[vmem] * 3,...  1.58 us

profile of v2, /device:TPU:0, one launch (start us, length us, event | category | flops | bytes accessed | tf_op | source)
XLA Modules:
  0.0 34.8 jit_solution(2637005849611074172)
XLA Ops:
  1.3 32.0 %correlate.1 = (f32[128,128]{1,0:T(8,128)}, f32[128,128]{1,0:T(8,128)}, f32[128,128]{1,0:T(8,128)}) custom-call(f32[1]{0:T(128)S(6)} %copy.9.defocus, s32[4]{0:T(128)} %index.1, bf16[128,512]{1,0:T(8,128)(2,1)} %mic_hbm.1, bf16[20,128,512]{2,1,0:T(8,128)(2,1)} %bank_hbm.1, f32[512,512]{1,0:T(8,128)} %noise_hbm.1, bf16[512,1536]{1,0:T(8,128)(2,1)} %constant.2.clone.table_hbm), custom_call_target="tpu_custom_call" | custom-call | tf_op jit(solution)/shard_map/correlate/pallas_call | solution.py:319
  33.3 1.6 %write_out.1 = (f32[128,128]{1,0:T(8,128)}, f32[128,128]{1,0:T(8,128)}, f32[128,128]{1,0:T(8,128)}) custom-call(f32[128,128]{1,0:T(8,128)} %get-tuple-element.6.peak_in, f32[128,128]{1,0:T(8,128)} %get-tuple-element.7.total_in, f32[128,128]{1,0:T(8,128)} %get-tuple-element.8.squares_in), custom_call_target="tpu_custom_call" | custom-call | tf_op jit(solution)/shard_map/write_out/pallas_call | solution.py:347

commit v3 on v2

--- a/solution.py
+++ b/solution.py
@@ -105,7 +105,7 @@
 
 
 def kernel(n, m, size, defocus, index, mic_hbm, bank_hbm, noise_hbm, table_hbm, peak, total, squares,
-           bank, chosen, mic, noise, table, mics, halves, beside, tmp_mic, tmp, proj_re, proj_im, cross, half, stage, inbox, part,
+           bank, chosen, mic, noise, table, mics, halves, beside, tmp_mic, tmp, spec_re, spec_im, proj_re, proj_im, cross, half, stage, inbox, part,
            local_sem, near, out_send, out_recv):
     row = lax.axis_index("rows")
     col = lax.axis_index("orient")
@@ -197,6 +197,24 @@
     for g in range(size // step):
         rows_g = slice(g * step, (g + 1) * step)
         noise[rows_g, :] = (sin_y[rows_g] * left_x + cos_y[rows_g] * right_x) * lax.rsqrt(noise[rows_g, :])
+    home = (row // 2) * 2 * slab
+    away = (1 - row // 2) * 2 * slab
+
+    def rows_at(first):
+        return pl.ds(pl.multiple_of(first, 2 * slab), 2 * slab)
+
+    def partial_re(rows_g, first):
+        return dot(table[rows_g, rows_at(size + first)], tmp_mic[rows_at(first), :]) + dot(
+            table[rows_g, rows_at(2 * size + first)], tmp_mic[rows_at(size + first), :])
+
+    def partial_im(rows_g, first):
+        return dot(table[rows_g, rows_at(first)], tmp_mic[rows_at(first), :]) + dot(
+            table[rows_g, rows_at(size + first)], tmp_mic[rows_at(size + first), :])
+
+    for g in range(size // step):
+        rows_g = slice(g * step, (g + 1) * step)
+        spec_re[rows_g, :] = partial_re(rows_g, home)
+        spec_im[rows_g, :] = partial_im(rows_g, home)
     pass_over.wait_recv()
     row_dft(tmp, halves[0].reshape(slab, size), over)
     mic_over.wait_recv()
@@ -212,8 +230,8 @@
     row_dft(tmp_mic, mics[2], corner)
     for g in range(size // step):
         rows_g = slice(g * step, (g + 1) * step)
-        s_re = dot(table[rows_g, size:], tmp_mic[...])
-        s_im = dot(table[rows_g, :2 * size], tmp_mic[...])
+        s_re = spec_re[rows_g, :] + partial_re(rows_g, away)
+        s_im = spec_im[rows_g, :] + partial_im(rows_g, away)
         p_re = proj_re[rows_g, :]
         p_im = proj_im[rows_g, :]
         cross[rows_g, :] = (s_re * p_re + s_im * p_im).astype(jnp.bfloat16)
@@ -295,10 +313,16 @@
                     out_copy(kind, lax.rem(row + a, n), lax.rem(side + b, 2), me).wait_send()
 
 
-def write_out(peak_in, total_in, squares_in, peak, total, squares):
-    peak[...] = peak_in[...]
-    total[...] = total_in[...]
-    squares[...] = squares_in[...]
+def write_out(peak_in, total_in, squares_in, peak, total, squares, held, sems):
+    reads = [pltpu.make_async_copy(r, held.at[i], sems.at[0, i]) for i, r in enumerate((peak_in, total_in, squares_in))]
+    writes = [pltpu.make_async_copy(held.at[i], w, sems.at[1, i]) for i, w in enumerate((peak, total, squares))]
+    for copy in reads:
+        copy.start()
+    for read, write in zip(reads, writes):
+        read.wait()
+        write.start()
+    for copy in writes:
+        copy.wait()
 
 
 def local(micrograph, bank, orient_index, noise_power, defocus):
@@ -334,6 +358,8 @@
             pltpu.VMEM((2 * size, size), bf16),
             pltpu.VMEM((size, size), jnp.float32),
             pltpu.VMEM((size, size), jnp.float32),
+            pltpu.VMEM((size, size), jnp.float32),
+            pltpu.VMEM((size, size), jnp.float32),
             pltpu.VMEM((2 * size, size), bf16),
             pltpu.VMEM((n // 2, 2 * slab, 2 * size), bf16),
             pltpu.VMEM((2, 2 * n, slab, width), bf16),
@@ -347,8 +373,9 @@
     return pl.pallas_call(
         write_out,
         out_shape=(out, out, out),
-        in_specs=[vmem] * 3,
-        out_specs=(vmem, vmem, vmem),
+        in_specs=[hbm] * 3,
+        out_specs=(hbm, hbm, hbm),
+        scratch_shapes=[pltpu.VMEM((3, slab, width), jnp.float32), dma((2, 3))],
         name="write_out",
     )(*maps)
 

time: 35 us -> 34.6 us (0.989)
  Pallas kernels: 33.6 us -> 33.1 us
    pallas_call x1, Pallas kernels: 32 us -> 31.5 us  [local(): pl.pallas_call(functools.partial(kernel, n, m, size), out_shape=(out, out...]
where the time goes in v3:
time: 34.6 us; the launch traced here: 34.4 us
  Pallas kernels  33.1 us (96%)
  between operations  1.29 us (4%)
    pallas_call x1, Pallas kernels, local(): pl.pallas_call(functools.partial(kernel, n, m, size), out_shape=(out, out...  31.5 us
    pallas_call x1, Pallas kernels, local(): pl.pallas_call(write_out, out_shape=(out, out, out), in_specs=[hbm] * 3,...  1.58 us

profile of v3, /device:TPU:0, one launch (start us, length us, event | category | flops | bytes accessed | tf_op | source)
XLA Modules:
  0.0 34.4 jit_solution(638143505824891298)
XLA Ops:
  1.3 31.5 %correlate.1 = (f32[128,128]{1,0:T(8,128)}, f32[128,128]{1,0:T(8,128)}, f32[128,128]{1,0:T(8,128)}) custom-call(f32[1]{0:T(128)S(6)} %copy.9.defocus, s32[4]{0:T(128)} %index.1, bf16[128,512]{1,0:T(8,128)(2,1)} %mic_hbm.1, bf16[20,128,512]{2,1,0:T(8,128)(2,1)} %bank_hbm.1, f32[512,512]{1,0:T(8,128)} %noise_hbm.1, bf16[512,1536]{1,0:T(8,128)(2,1)} %constant.2.clone.table_hbm), custom_call_target="tpu_custom_call" | custom-call | tf_op jit(solution)/shard_map/correlate/pallas_call | solution.py:343
  32.8 1.6 %write_out.1 = (f32[128,128]{1,0:T(8,128)}, f32[128,128]{1,0:T(8,128)}, f32[128,128]{1,0:T(8,128)}) custom-call(f32[128,128]{1,0:T(8,128)} %get-tuple-element.6.peak_in, f32[128,128]{1,0:T(8,128)} %get-tuple-element.7.total_in, f32[128,128]{1,0:T(8,128)} %get-tuple-element.8.squares_in), custom_call_target="tpu_custom_call" | custom-call | tf_op jit(solution)/shard_map/write_out/pallas_call | solution.py:373
